TPU v7x, 128 devices: a whole 4x4x4 slice. The times are simulated.
128 devices in a mesh: req: 16 (over z, y), kv: 8 (over x, core).
Axes of the slice: x: 4, y: 4, z: 4, core: 2. Of those that a mesh axis runs over, the one named last changes fastest.
Arguments:
- hidden_in: bfloat16 [16384, 2048], P(('req', 'kv')), may hold values from -6 to 6
- slot_tokens: int32 [16384], replicated, may hold values from 0 to 16383, as said below
- cache_len: int32 [128], P('req'), may hold values from 1 to 2048, 65536 in all
- prefill_start: int32 [16], P('req'), may hold values from 0 to 2048
- key_cache: bfloat16 [128, 2048, 1024], P('req', None, 'kv')
- value_cache: bfloat16 [128, 2048, 1024], P('req', None, 'kv'), may hold values from -18 to 18
- key_prefix: bfloat16 [16, 2048, 1024], P('req', None, 'kv')
- value_prefix: bfloat16 [16, 2048, 1024], P('req', None, 'kv'), may hold values from -18 to 18
- attn_gain: float32 [2048], replicated, may hold values from 0.25 to 1.75
- q_proj: bfloat16 [2048, 2048], P(None, 'kv'), may hold values from -0.125 to 0.125
- k_proj: bfloat16 [2048, 1024], P(None, 'kv'), may hold values from -0.125 to 0.125
- v_proj: bfloat16 [2048, 1024], P(None, 'kv'), may hold values from -0.125 to 0.125
- q_gain: float32 [128], replicated, may hold values from 0.25 to 1.75
- k_gain: float32 [128], replicated, may hold values from 0.25 to 1.75
- o_proj: bfloat16 [2048, 2048], P('kv'), may hold values from -0.125 to 0.125
- ffn_gain: float32 [2048], replicated, may hold values from 0.25 to 1.75
- w_gate: bfloat16 [2048, 6144], P(None, 'req'), may hold values from -0.125 to 0.125
- w_up: bfloat16 [2048, 6144], P(None, 'req'), may hold values from -0.125 to 0.125
- w_down: bfloat16 [6144, 2048], P('req'), may hold values from -0.078125 to 0.078125
- final_gain: float32 [2048], replicated, may hold values from 0.25 to 1.75
- lm_head: bfloat16 [2048, 151936], P(None, ('req', 'kv')), may hold values from -0.375 to 0.375
Outputs:
- layer_out: bfloat16 [16384, 2048], P(('req', 'kv'))
- max_logit: float32 [144], replicated
Inputs may be any that keep to these rules, and one draw needn't show every extreme that they name: slot_tokens is a permutation of the batch's tokens; each device's 128 consecutive slots take exactly 1 token from each device's 128 consecutive batch tokens.
All inputs are finite; a program needn't handle non-finite values. No bound on the sum of `cache_len` on one device may be relied on, other than what follows from the above.
Results may differ from a plain program's by a relative error of at most 0.0085.
The roundings to bfloat16 on the way count: a program that leaves them out, or rounds other values in their place, can miss the bound.
Values may be sent and summed in bfloat16 or wider, within the bound.
A program may use at most 128 MiB of HBM per device.

v0:
```python
import jax
import jax.numpy as jnp
from jax import lax
from jax.sharding import PartitionSpec as P

EPS = 1e-06
NEG = -1e30


def spread(value, axis, root):
    mine = lax.axis_index(axis) == root
    return lax.psum(jnp.where(mine, value, jnp.zeros_like(value)), axis)


def norm_rows(values, gain_vec):
    wide = values.astype(jnp.float32)
    return wide * lax.rsqrt(jnp.mean(wide * wide, axis=-1, keepdims=True) + EPS) * gain_vec


def rotate(values, places):
    half_dim = values.shape[-1] // 2
    freqs = 1000000.0 ** (-(jnp.arange(half_dim, dtype=jnp.float32) * 2.0 / values.shape[-1]))
    angles = places[:, None] * freqs[None, :]
    cosine = jnp.cos(angles)[:, None, :]
    sine = jnp.sin(angles)[:, None, :]
    first_half = values[..., :half_dim]
    second_half = values[..., half_dim:]
    return jnp.concatenate(
        [first_half * cosine - second_half * sine, second_half * cosine + first_half * sine],
        axis=-1,
    )


def prefill_full(q_heads, key_old, value_old, key_new, value_new, start_at):
    old_len = key_old.shape[0]
    fresh_rows = q_heads.shape[0]
    factor = q_heads.shape[-1] ** (-0.5)
    all_keys = jnp.concatenate([key_old, key_new], axis=0)
    all_values = jnp.concatenate([value_old, value_new], axis=0)
    scores = (
        jnp.einsum("cgd,kd->gck", q_heads, all_keys, preferred_element_type=jnp.float32) * factor
    )
    key_index = jnp.arange(old_len + fresh_rows, dtype=jnp.int32)[None, :]
    row_index = jnp.arange(fresh_rows, dtype=jnp.int32)[:, None]
    allowed = jnp.where(key_index < old_len, key_index < start_at, key_index - old_len <= row_index)
    scores = jnp.where(allowed[None], scores, NEG)
    row_peak = jnp.max(scores, axis=-1, keepdims=True)
    expd = jnp.exp(scores - row_peak)
    weights = (expd / jnp.sum(expd, axis=-1, keepdims=True)).astype(jnp.bfloat16)
    return jnp.einsum(
        "gck,kd->cgd", weights, all_values, preferred_element_type=jnp.float32
    ).astype(jnp.bfloat16)


def decode_attend(q_heads, key_old, value_old, key_self, value_self, lengths):
    factor = q_heads.shape[-1] ** (-0.5)
    past = jnp.einsum("bgd,bld->bgl", q_heads, key_old, preferred_element_type=jnp.float32) * factor
    slot_index = jnp.arange(key_old.shape[1], dtype=jnp.int32)
    past = jnp.where(slot_index[None, None, :] < lengths[:, None, None], past, NEG)
    own_score = (
        jnp.einsum("bgd,bd->bg", q_heads, key_self, preferred_element_type=jnp.float32) * factor
    )
    row_peak = jnp.maximum(jnp.max(past, axis=-1), own_score)
    past_exp = jnp.exp(past - row_peak[..., None])
    own_exp = jnp.exp(own_score - row_peak)
    row_total = jnp.sum(past_exp, axis=-1) + own_exp
    past_w = (past_exp / row_total[..., None]).astype(jnp.bfloat16)
    own_w = (own_exp / row_total).astype(jnp.bfloat16)
    summed = jnp.einsum("bgl,bld->bgd", past_w, value_old, preferred_element_type=jnp.float32)
    summed = (
        summed + own_w.astype(jnp.float32)[..., None] * value_self.astype(jnp.float32)[:, None, :]
    )
    return summed.astype(jnp.bfloat16)


def butterfly(value, axis, combine):
    size = lax.axis_size(axis)
    step = 1
    while step < size:
        pairs = [(i, i ^ step) for i in range(size)]
        value = combine(value, lax.ppermute(value, axis, pairs))
        step *= 2
    return value


def butterfly_gather(value, axis):
    size = lax.axis_size(axis)
    me = lax.axis_index(axis)
    step = 1
    while step < size:
        pairs = [(i, i ^ step) for i in range(size)]
        other = lax.ppermute(value, axis, pairs)
        low = me // step % 2 == 0
        value = jnp.concatenate(
            [jnp.where(low, value, other), jnp.where(low, other, value)], axis=0
        )
        step *= 2
    return value


def radix_exchange(value, axis, step, radix):
    size = lax.axis_size(axis)
    got = [value]
    for digit in range(1, radix):
        pairs = [(i, i ^ digit * step) for i in range(size)]
        got.append(lax.ppermute(value, axis, pairs))
    return got


def radix_reduce(value, axis, combine, radix):
    size = lax.axis_size(axis)
    step = 1
    while step < size:
        for other in radix_exchange(value, axis, step, radix)[1:]:
            value = combine(value, other)
        step *= radix
    return value


def radix_gather(value, axis, radix):
    size = lax.axis_size(axis)
    me = lax.axis_index(axis)
    step = 1
    while step < size:
        got = radix_exchange(value, axis, step, radix)
        order = jnp.arange(radix, dtype=jnp.int32) ^ me // step % radix
        value = jnp.stack(got)[order].reshape((radix * value.shape[0],) + value.shape[1:])
        step *= radix
    return value


def mixed_reduce(value, axis, combine, radices):
    me = lax.axis_index(axis)
    step = 1
    for radix in radices:
        got = radix_exchange(value, axis, step, radix)
        order = jnp.arange(radix, dtype=jnp.int32) ^ me // step % radix
        members = jnp.stack(got)[order]
        while members.shape[0] > 1:
            members = combine(members[0::2], members[1::2])
        value = members[0]
        step *= radix
    return value


def regroup(rows_in):
    return lax.all_to_all(rows_in, ("req", "kv"), split_axis=0, concat_axis=0, tiled=True)


def shards(
    hidden_in,
    slot_tokens,
    cache_len,
    prefill_start,
    key_cache,
    value_cache,
    key_prefix,
    value_prefix,
    attn_gain,
    q_proj,
    k_proj,
    v_proj,
    q_gain,
    k_gain,
    o_proj,
    ffn_gain,
    w_gate,
    w_up,
    w_down,
    final_gain,
    lm_head,
):
    req_count = lax.axis_size("req")
    kv_count = lax.axis_size("kv")
    devices = req_count * kv_count
    rows_dev = hidden_in.shape[0]
    kv_index = lax.axis_index("kv")
    self_index = lax.axis_index("req") * kv_count + kv_index
    slot_table = slot_tokens.reshape(devices, rows_dev)
    from_self = slot_table // rows_dev == self_index
    send_rows = jnp.sum(jnp.where(from_self, slot_table - self_index * rows_dev, 0), axis=1)
    slot_place = lax.dynamic_index_in_dim(slot_table, self_index, 0, keepdims=False) // rows_dev
    arrived = regroup(hidden_in[send_rows])
    owner_rows = arrived[slot_place]
    rows_all = lax.all_gather(owner_rows, "kv", axis=0, tiled=True)
    normed = norm_rows(rows_all, attn_gain).astype(jnp.bfloat16)
    o_full = lax.all_to_all(
        jnp.broadcast_to(o_proj[None], (kv_count,) + o_proj.shape),
        "kv",
        split_axis=0,
        concat_axis=0,
        tiled=True,
    ).reshape(kv_count * o_proj.shape[0], o_proj.shape[1])
    ff_dev = w_gate.shape[1]
    ff_piece = ff_dev // kv_count
    weight_piece = jnp.stack(
        [
            lax.dynamic_slice_in_dim(w_gate, kv_index * ff_piece, ff_piece, axis=1).T,
            lax.dynamic_slice_in_dim(w_up, kv_index * ff_piece, ff_piece, axis=1).T,
            lax.dynamic_slice_in_dim(w_down, kv_index * ff_piece, ff_piece, axis=0),
        ]
    )
    weight_all = lax.all_gather(weight_piece, "req", axis=1, tiled=True)
    model_dim = w_gate.shape[0]
    q_cols = q_proj.shape[1]
    kv_cols = k_proj.shape[1]
    projected = jnp.concatenate(
        [
            jnp.dot(normed, q_proj, preferred_element_type=jnp.float32),
            jnp.dot(normed, k_proj, preferred_element_type=jnp.float32),
            jnp.dot(normed, v_proj, preferred_element_type=jnp.float32),
        ],
        axis=1,
    )
    tok_req = projected.shape[0]
    head_dim = q_gain.shape[0]
    dec_count = cache_len.shape[0]
    fresh_count = tok_req - dec_count
    q_raw = projected[:, :q_cols].reshape(tok_req, q_cols // head_dim, head_dim)
    k_raw = projected[:, q_cols : q_cols + kv_cols].reshape(tok_req, kv_cols // head_dim, head_dim)
    v_new = (
        projected[:, q_cols + kv_cols :]
        .astype(jnp.bfloat16)
        .reshape(tok_req, kv_cols // head_dim, head_dim)
    )
    places = jnp.concatenate(
        [prefill_start[0] + jnp.arange(fresh_count, dtype=jnp.int32), cache_len]
    ).astype(jnp.float32)
    queries = rotate(norm_rows(q_raw, q_gain), places).astype(jnp.bfloat16)
    keys_new = rotate(norm_rows(k_raw, k_gain), places).astype(jnp.bfloat16)
    pre_out = prefill_full(
        queries[:fresh_count],
        key_prefix[0, :, 0:head_dim],
        value_prefix[0, :, 0:head_dim],
        keys_new[:fresh_count, 0],
        v_new[:fresh_count, 0],
        prefill_start[0],
    )
    dec_out = decode_attend(
        queries[fresh_count:],
        key_cache,
        value_cache,
        keys_new[fresh_count:, 0],
        v_new[fresh_count:, 0],
        cache_len,
    )
    pieces = jnp.concatenate([pre_out, dec_out], axis=0)
    pieces, weight_all, o_full = lax.optimization_barrier((pieces, weight_all, o_full))
    gate_w = weight_all[0]
    up_w = weight_all[1]
    down_w = weight_all[2]
    attended = lax.all_gather(pieces.reshape(tok_req, q_cols), "kv", axis=1, tiled=True)
    resid = (
        rows_all.astype(jnp.float32) + jnp.dot(attended, o_full, preferred_element_type=jnp.float32)
    ).astype(jnp.bfloat16)
    ffn_in = norm_rows(resid, ffn_gain).astype(jnp.bfloat16)
    contract_last = (((1,), (1,)), ((), ()))
    gate_part = lax.dot_general(ffn_in, gate_w, contract_last, preferred_element_type=jnp.float32)
    up_part = lax.dot_general(ffn_in, up_w, contract_last, preferred_element_type=jnp.float32)
    hidden_act = (jax.nn.silu(gate_part) * up_part).astype(jnp.bfloat16)
    tail_count = tok_req - fresh_count + 1
    tail_pad = -(-tail_count // 8) * 8
    down_part = jnp.dot(hidden_act, down_w, preferred_element_type=jnp.float32)
    ffn_part = lax.psum_scatter(down_part, "kv", scatter_dimension=0, tiled=True)
    tail_part = jnp.dot(
        hidden_act[tok_req - tail_pad :], down_w, preferred_element_type=jnp.float32
    )
    tail_sum = mixed_reduce(tail_part, "kv", jnp.add, (2, 4))[tail_pad - tail_count :]
    tail_out = (resid[fresh_count - 1 :].astype(jnp.float32) + tail_sum).astype(jnp.bfloat16)
    tail_rows = norm_rows(tail_out, final_gain).astype(jnp.bfloat16)
    local_peaks = jnp.max(
        jnp.dot(radix_gather(tail_rows, "req", 4), lm_head, preferred_element_type=jnp.float32),
        axis=1,
    )
    max_logit = radix_reduce(
        mixed_reduce(local_peaks, "kv", jnp.maximum, (2, 4)), "req", jnp.maximum, 4
    )
    ffn_part, max_logit = lax.optimization_barrier((ffn_part, max_logit))
    mine = lax.dynamic_slice_in_dim(resid, kv_index * rows_dev, rows_dev, axis=0)
    out_rows = (mine.astype(jnp.float32) + ffn_part).astype(jnp.bfloat16)
    going_back = jnp.zeros_like(out_rows).at[slot_place].set(out_rows)
    returned = regroup(going_back)
    layer_out = jnp.zeros_like(hidden_in).at[send_rows].set(returned)
    return (layer_out, max_logit)


def solution(mesh):
    placed = (
        P(("req", "kv"), None),
        P(),
        P("req"),
        P("req"),
        P("req", None, "kv"),
        P("req", None, "kv"),
        P("req", None, "kv"),
        P("req", None, "kv"),
        P(),
        P(None, "kv"),
        P(None, "kv"),
        P(None, "kv"),
        P(),
        P(),
        P("kv", None),
        P(),
        P(None, "req"),
        P(None, "req"),
        P("req", None),
        P(),
        P(None, ("req", "kv")),
    )
    return jax.shard_map(
        shards, mesh=mesh, in_specs=placed, out_specs=(P(("req", "kv"), None), P()), check_vma=False
    )
```

profile of v0, /device:TPU:1, one launch (start us, length us, event | category | flops | bytes accessed | tf_op | source)
XLA Modules:
  0.0 336.4 jit_solution(1163954709671219122)
XLA Ops:
  8.3 2.6 gather_fusion
  13.5 11.5 %all-to-all-start = ((bf16[128,2,1024]{2,1,0:T(2,128)(2,1)}), bf16[128,2,1024]{2,1,0:T(2,128)(2,1)S(1)}, u32[]{:S(2)}, u32[]{:S(2)}) async-start(bf16[128,2,1024]{2,1,0:T(2,128)(2,1)} %reshape.574), calls=%async_computation | async-start | bytes 1048576 | tf_op jit(solution)/shard_map/all_to_all | solution.py:147
  25.8 13.0 %all-to-all-done = bf16[128,2,1024]{2,1,0:T(2,128)(2,1)S(1)} async-done(((bf16[128,2,1024]{2,1,0:T(2,128)(2,1)}), bf16[128,2,1024]{2,1,0:T(2,128)(2,1)S(1)}, u32[]{:S(2)}, u32[]{:S(2)}) %all-to-all-start) | async-done | bytes 524320 | tf_op jit(solution)/shard_map/all_to_all | solution.py:147
  44.6 5.6 %broadcast_in_dim.46 = bf16[8,256,2048]{2,1,0:T(8,128)(2,1)} broadcast(bf16[256,2048]{1,0:T(8,128)(2,1)} %param.35), dimensions={1,2} | broadcast | bytes 9437184 | tf_op jit(solution)/shard_map/broadcast_in_dim | solution.py:188
  50.2 5.8 %all-to-all-start.1 = ((bf16[8,256,2048]{2,1,0:T(8,128)(2,1)}), bf16[8,256,2048]{2,1,0:T(8,128)(2,1)}, u32[]{:S(2)}, u32[]{:S(2)}) async-start(bf16[8,256,2048]{2,1,0:T(8,128)(2,1)} %broadcast_in_dim.46), calls=%async_computation.1 | async-start | bytes 16777216 | tf_op jit(solution)/shard_map/all_to_all | solution.py:187
  59.0 4.0 %fusion.4 = pred[1016,3064]{1,0:T(8,128)(4,1)} fusion(s32[3064]{0:T(1024)S(1)} %iota_add_fusion, pred[3064]{0:T(1024)(128)(4,1)S(1)} %get-tuple-element.34, pred[3064]{0:T(1024)(128)(4,1)S(1)} %get-tuple-element.35), kind=kLoop, calls=%fused_computation.21 | loop fusion | flops 6226048 | bytes 3131408 | tf_op jit(solution)/shard_map/jit(_where)/select_n | solution.py:45
  63.1 23.5 %all-gather.9.cloned.1.call-done = bf16[1024,2048]{1,0:T(8,128)(2,1)} async-done(((bf16[128,2048]{1,0:T(8,128)(2,1)}), bf16[1024,2048]{1,0:T(8,128)(2,1)}) %all-gather.9.cloned.1.call-update) | async-done | bytes 4194320 | tf_op jit(solution)/shard_map/all_gather | solution.py:185
  86.6 3.2 fusion.10
  91.3 2.3 multiply_reduce_fusion
  95.2 3.7 %multiply_reduce_fusion.1 = (f32[1024]{0:T(1024)S(1)}, f32[1024,128]{0,1:T(8,128)S(1)}) fusion(bf16[1024,2048]{1,0:T(8,128)(2,1)} %copy-done.3, bf16[2048,128]{1,0:T(8,128)(2,1)S(1)} %copy-done.6), kind=kOutput, calls=%fused_computation.77 | convolution fusion | flops 537132032 | bytes 5246976 | tf_op jit(solution)/shard_map/dot_general | solution.py:210
  104.7 3.9 %convolution_convert_fusion = bf16[1024,128]{1,0:T(8,128)(2,1)S(1)} fusion(bf16[1024,2048]{1,0:T(8,128)(2,1)} %copy-done.3, bf16[2048,128]{1,0:T(8,128)(2,1)S(1)} %copy-done.14), kind=kOutput, calls=%fused_computation.51 | convolution fusion | flops 537001984 | bytes 4980736 | tf_op jit(solution)/shard_map/dot_general | solution.py:211
  109.5 15.9 %fusion.96 = (f32[2,1016]{1,0:T(2,128)S(1)}, f32[2,1016,3064]{2,1,0:T(8,128)}) fusion(pred[1016,3064]{1,0:T(8,128)(4,1)} %fusion.4, bf16[1016,128]{1,0:T(8,128)(2,1)S(1)} %copy.49, bf16[2048,128]{1,0:T(8,128)(2,1)S(1)} %bitcast.175, bf16[1024,2,64]{2,0,1:T(8,128)(2,1)S(1)} %get-tuple-element.14, bf16[1024,2,64]{2,0,1:T(8,128)(2,1)S(1)} %get-tuple-element.15), kind=kOutput, calls=%fused_computation.188 | convolution fusion | flops 1621384704 | bytes 29334016 | tf_op jit(solution)/shard_map/sub | solution.py:48
  125.4 12.3 %fusion.32 = bf16[1016,2,128]{2,0,1:T(8,128)(2,1)S(1)} fusion(f32[2,1016,3064]{2,1,0:T(8,128)} %get-tuple-element.31, f32[2,1016]{1,0:T(2,128)S(1)} %get-tuple-element.30, bf16[1016,128]{1,0:T(8,128)(2,1)S(1)} %slice.142, bf16[2048,128]{1,0:T(8,128)(2,1)S(1)} %bitcast.176), kind=kOutput, calls=%fused_computation.50 | convolution fusion | flops 1608149248 | bytes 26216896 | tf_op jit(solution)/shard_map/gck,kd->cgd/dot_general | solution.py:50
  137.8 20.7 %all-to-all-done.1 = bf16[8,256,2048]{2,1,0:T(8,128)(2,1)} async-done(((bf16[8,256,2048]{2,1,0:T(8,128)(2,1)}), bf16[8,256,2048]{2,1,0:T(8,128)(2,1)}, u32[]{:S(2)}, u32[]{:S(2)}) %all-to-all-start.1) | async-done | bytes 8388640 | tf_op jit(solution)/shard_map/all_to_all | solution.py:187
  158.4 12.4 %all-gather.5.cloned.1.call-done = bf16[3,768,2048]{2,1,0:T(8,128)(2,1)} async-done(((bf16[3,48,2048]{2,1,0:T(8,128)(2,1)}), bf16[3,768,2048]{2,1,0:T(8,128)(2,1)}) %all-gather.5.cloned.1.call-update) | async-done | bytes 9437200 | tf_op jit(solution)/shard_map/all_gather | solution.py:203
  171.9 33.3 %all-gather.7.cloned.1.call-done = bf16[1024,2048]{0,1:T(8,128)(2,1)} async-done(((bf16[1024,256]{0,1:T(8,128)(2,1)}), bf16[1024,2048]{0,1:T(8,128)(2,1)}) %all-gather.7.cloned.1.call-update) | async-done | bytes 4194320 | tf_op jit(solution)/shard_map/all_gather | solution.py:252
  205.2 14.6 %fusion.7 = (f32[1024]{0:T(1024)S(1)}, bf16[1024,2048]{1,0:T(8,128)(2,1)S(1)}) fusion(bf16[1024,2048]{0,1:T(8,128)(2,1)} %all-gather.7.cloned.1.call-done, bf16[2048,2048]{1,0:T(8,128)(2,1)} %bitcast.25, bf16[1024,2048]{1,0:T(8,128)(2,1)} %all-gather.9.cloned.1.call-done), kind=kOutput, calls=%fused_computation.26 | convolution fusion | flops 8602516480 | bytes 20975616 | tf_op jit(solution)/shard_map/dot_general | solution.py:254
  219.9 7.0 %fusion.18 = f32[1024,768]{1,0:T(8,128)S(1)} fusion(bf16[3,768,2048]{2,1,0:T(8,128)(2,1)} %all-gather.5.cloned.1.call-done, bf16[1024,2048]{1,0:T(8,128)(2,1)S(1)} %get-tuple-element.33, f32[2048]{0:T(1024)S(1)} %copy-done.17, f32[1024]{0:T(1024)S(1)} %add_rsqrt_fusion.1), kind=kOutput, calls=%fused_computation.37 | convolution fusion | flops 3229614080 | bytes 10498048 | tf_op jit(solution)/shard_map/dot_general | solution.py:259
  227.0 3.9 %multiply_convert_fusion = bf16[1024,768]{1,0:T(8,128)(2,1)S(1)} fusion(f32[1024,768]{1,0:T(8,128)S(1)} %fusion.18, bf16[3,768,2048]{2,1,0:T(8,128)(2,1)S(1)} %bitcast.145, bf16[1024,2048]{1,0:T(8,128)(2,1)S(1)} %get-tuple-element.33, f32[2048]{0:T(1024)S(1)} %copy-done.17, f32[1024]{0:T(1024)S(1)} %add_rsqrt_fusion.1), kind=kOutput, calls=%fused_computation.41 | convolution fusion | flops 3234332672 | bytes 12070912 | tf_op jit(solution)/shard_map/dot_general | solution.py:258
  230.9 5.6 %fusion.16 = f32[1024,2048]{1,0:T(8,128)} fusion(bf16[1024,768]{1,0:T(8,128)(2,1)S(1)} %multiply_convert_fusion, bf16[3,768,2048]{2,1,0:T(8,128)(2,1)S(1)} %bitcast.145), kind=kOutput, calls=%fused_computation.35 | convolution fusion | flops 3221225472 | bytes 13107200 | tf_op jit(solution)/shard_map/dot_general | solution.py:263
  236.7 2.4 fusion.14
  244.6 6.2 %collective-permute-done.3 = f32[16,2048]{1,0:T(8,128)S(1)} collective-permute-done((f32[16,2048]{1,0:T(8,128)S(1)}, f32[16,2048]{1,0:T(8,128)S(1)}, u32[]{:S(2)}, u32[]{:S(2)}) %collective-permute-start.3) | collective-permute-done | bytes 131104 | tf_op jit(solution)/shard_map/ppermute | solution.py:106
  253.9 2.5 collective-permute-start.6
  258.7 2.4 collective-permute-done.5
  261.8 2.7 collective-permute-start.9
  265.3 3.3 collective-permute-done.9
  271.2 4.3 %convolution_reduce_fusion = f32[144]{0:T(256)S(1)} fusion(bf16[144,2048]{1,0:T(8,128)(2,1)S(1)} %reshape.484, bf16[2048,1187]{0,1:T(8,128)(2,1)} %param.41), kind=kOutput, calls=%fused_computation.52 | convolution fusion | flops 700291840 | bytes 5452352 | tf_op jit(solution)/shard_map/dot_general | solution.py:272
  275.4 5.0 %collective-permute-start.10 = (f32[144]{0:T(256)S(1)}, f32[144]{0:T(256)S(1)}, u32[]{:S(2)}, u32[]{:S(2)}) collective-permute-start(f32[144]{0:T(256)S(1)} %convolution_reduce_fusion), channel_id=1, source_target_pairs={{0,1},{1,0},{2,3},{3,2},{4,5},{5,4},{6,7},{7,6},{8,9},{9,8},{10,11... | collective-permute-start | bytes 1736 | tf_op jit(solution)/shard_map/ppermute | solution.py:106
  296.4 2.3 collective-permute-done.18
  299.4 2.3 scatter_custom_fusion
  303.1 23.8 %all_to_all.29 = bf16[128,2,1024]{2,1,0:T(2,128)(2,1)S(1)} all-to-all(bf16[128,2,1024]{2,1,0:T(2,128)(2,1)S(1)} %reshape.576), channel_id=1, replica_groups=mesh['req'=16,'kv'=8] {'req','kv'}, dimensions={0} | all-to-all | bytes 1048576 | tf_op jit(solution)/shard_map/all_to_all | solution.py:147
  327.3 2.4 scatter_custom_fusion.1
  (176 shorter events, 56.4 us)
Async XLA Ops:
  7.2 36.5 %copy-start = (bf16[384,2048]{1,0:T(8,128)(2,1)S(1)}, bf16[384,2048]{1,0:T(8,128)(2,1)}, u32[]{:S(2)}) copy-start(bf16[384,2048]{1,0:T(8,128)(2,1)} %param.39) | copy-start | bytes 4718596
  13.5 25.2 %all-to-all-start = ((bf16[128,2,1024]{2,1,0:T(2,128)(2,1)}), bf16[128,2,1024]{2,1,0:T(2,128)(2,1)S(1)}, u32[]{:S(2)}, u32[]{:S(2)}) async-start(bf16[128,2,1024]{2,1,0:T(2,128)(2,1)} %reshape.574), calls=%async_computation | async-start | bytes 1048576 | tf_op jit(solution)/shard_map/all_to_all | solution.py:147
  25.0 61.6 %all-gather.9.cloned.1.call-start = ((), (), s32[]{:S(2)}) async-start(), calls=%async_computation.7 | async-start | bytes 4718592 | tf_op jit(solution)/shard_map/all_gather | solution.py:185
  41.3 129.5 %all-gather.5.cloned.1.call-start = ((), (), s32[]{:S(2)}) async-start(), calls=%async_computation.4 | async-start | bytes 10027008 | tf_op jit(solution)/shard_map/all_gather | solution.py:203
  50.2 108.2 %all-to-all-start.1 = ((bf16[8,256,2048]{2,1,0:T(8,128)(2,1)}), bf16[8,256,2048]{2,1,0:T(8,128)(2,1)}, u32[]{:S(2)}, u32[]{:S(2)}) async-start(bf16[8,256,2048]{2,1,0:T(8,128)(2,1)} %broadcast_in_dim.46), calls=%async_computation.1 | async-start | bytes 16777216 | tf_op jit(solution)/shard_map/all_to_all | solution.py:187
  56.1 149.1 %all-gather.7.cloned.1.call-start = ((), (), s32[]{:S(2)}) async-start(), calls=%async_computation.5 | async-start | bytes 4718592 | tf_op jit(solution)/shard_map/all_gather | solution.py:252
  57.0 32.8 %copy-start.9 = (f32[2048]{0:T(1024)S(1)}, f32[2048]{0:T(1024)}, u32[]{:S(2)}) copy-start(f32[2048]{0:T(1024)} %param.29) | copy-start | bytes 24580
  171.8 48.0 %copy-start.17 = (f32[2048]{0:T(1024)S(1)}, f32[2048]{0:T(1024)}, u32[]{:S(2)}) copy-start(f32[2048]{0:T(1024)} %param.36) | copy-start | bytes 24580
  171.9 127.5 %reduce-scatter.2.cloned.1.call-start = ((), (), s32[]{:S(2)}) async-start(), calls=%async_computation.6 | async-start | bytes 9437184 | tf_op jit(solution)/shard_map/reduce_scatter | solution.py:264
  205.2 21.7 %slice-start = ((s8[9437184]{0:T(1024)(128)(4,1)}), s8[1048576]{0:T(1024)(128)(4,1)S(1)}, s32[]{:S(2)}) async-start(s8[9437184]{0:T(1024)(128)(4,1)} %bitcast.144), calls=%async_computation.8 | async-start | bytes 2097152
  205.2 21.7 %slice-start.1 = ((s8[9437184]{0:T(1024)(128)(4,1)}), s8[4194304]{0:T(1024)(128)(4,1)S(1)}, s32[]{:S(2)}) async-start(s8[9437184]{0:T(1024)(128)(4,1)} %bitcast.144), calls=%async_computation.9 | async-start | bytes 8388608
  239.1 1.5 collective-permute-start
  241.2 9.6 %collective-permute-start.3 = (f32[16,2048]{1,0:T(8,128)S(1)}, f32[16,2048]{1,0:T(8,128)S(1)}, u32[]{:S(2)}, u32[]{:S(2)}) collective-permute-start(f32[16,2048]{1,0:T(8,128)S(1)} %fusion.116), channel_id=1, source_target_pairs={{0,6},{1,7},{2,4},{3,5},{4,2},{5,3},{6,0},{7,1},{8,14},{9,15},{10,... | collective-permute-start | bytes 393224 | tf_op jit(solution)/shard_map/ppermute | solution.py:106
  241.8 8.9 %collective-permute-start.2 = (f32[16,2048]{1,0:T(8,128)S(1)}, f32[16,2048]{1,0:T(8,128)S(1)}, u32[]{:S(2)}, u32[]{:S(2)}) collective-permute-start(f32[16,2048]{1,0:T(8,128)S(1)} %fusion.116), channel_id=1, source_target_pairs={{0,4},{1,5},{2,6},{3,7},{4,0},{5,1},{6,2},{7,3},{8,12},{9,13},{10,... | collective-permute-start | bytes 393224 | tf_op jit(solution)/shard_map/ppermute | solution.py:106
  243.2 8.9 %collective-permute-start.1 = (f32[16,2048]{1,0:T(8,128)S(1)}, f32[16,2048]{1,0:T(8,128)S(1)}, u32[]{:S(2)}, u32[]{:S(2)}) collective-permute-start(f32[16,2048]{1,0:T(8,128)S(1)} %fusion.116), channel_id=1, source_target_pairs={{0,2},{1,3},{2,0},{3,1},{4,6},{5,7},{6,4},{7,5},{8,10},{9,11},{10,... | collective-permute-start | bytes 393224 | tf_op jit(solution)/shard_map/ppermute | solution.py:106
  253.9 4.8 %collective-permute-start.6 = (bf16[9,2048]{1,0:T(8,128)(2,1)S(1)}, bf16[9,2048]{1,0:T(8,128)(2,1)S(1)}, u32[]{:S(2)}, u32[]{:S(2)}) collective-permute-start(bf16[9,2048]{1,0:T(8,128)(2,1)S(1)} %fusion.56), channel_id=1, source_target_pairs={{0,24},{8,16},{16,8},{24,0},{32,56},{40,48},{48,40},{56,32},{64,88... | collective-permute-start | bytes 110600 | tf_op jit(solution)/shard_map/ppermute | solution.py:106
  256.4 4.7 %collective-permute-start.5 = (bf16[9,2048]{1,0:T(8,128)(2,1)S(1)}, bf16[9,2048]{1,0:T(8,128)(2,1)S(1)}, u32[]{:S(2)}, u32[]{:S(2)}) collective-permute-start(bf16[9,2048]{1,0:T(8,128)(2,1)S(1)} %fusion.56), channel_id=1, source_target_pairs={{0,16},{8,24},{16,0},{24,8},{32,48},{40,56},{48,32},{56,40},{64,80... | collective-permute-start | bytes 110600 | tf_op jit(solution)/shard_map/ppermute | solution.py:106
  257.0 4.2 %collective-permute-start.4 = (bf16[9,2048]{1,0:T(8,128)(2,1)S(1)}, bf16[9,2048]{1,0:T(8,128)(2,1)S(1)}, u32[]{:S(2)}, u32[]{:S(2)}) collective-permute-start(bf16[9,2048]{1,0:T(8,128)(2,1)S(1)} %fusion.56), channel_id=1, source_target_pairs={{0,8},{8,0},{16,24},{24,16},{32,40},{40,32},{48,56},{56,48},{64,72... | collective-permute-start | bytes 110600 | tf_op jit(solution)/shard_map/ppermute | solution.py:106
  261.8 6.8 %collective-permute-start.9 = (bf16[36,2048]{1,0:T(8,128)(2,1)S(1)}, bf16[36,2048]{1,0:T(8,128)(2,1)S(1)}, u32[]{:S(2)}, u32[]{:S(2)}) collective-permute-start(bf16[36,2048]{1,0:T(8,128)(2,1)S(1)} %reshape.483), channel_id=1, source_target_pairs={{0,96},{8,104},{16,112},{24,120},{32,64},{40,72},{48,80},{56,88},{... | collective-permute-start | bytes 442376 | tf_op jit(solution)/shard_map/ppermute | solution.py:106
  264.6 5.7 %collective-permute-start.8 = (bf16[36,2048]{1,0:T(8,128)(2,1)S(1)}, bf16[36,2048]{1,0:T(8,128)(2,1)S(1)}, u32[]{:S(2)}, u32[]{:S(2)}) collective-permute-start(bf16[36,2048]{1,0:T(8,128)(2,1)S(1)} %reshape.483), channel_id=1, source_target_pairs={{0,64},{8,72},{16,80},{24,88},{32,96},{40,104},{48,112},{56,120},{... | collective-permute-start | bytes 442376 | tf_op jit(solution)/shard_map/ppermute | solution.py:106
  265.0 5.3 %collective-permute-start.7 = (bf16[36,2048]{1,0:T(8,128)(2,1)S(1)}, bf16[36,2048]{1,0:T(8,128)(2,1)S(1)}, u32[]{:S(2)}, u32[]{:S(2)}) collective-permute-start(bf16[36,2048]{1,0:T(8,128)(2,1)S(1)} %reshape.483), channel_id=1, source_target_pairs={{0,32},{8,40},{16,48},{24,56},{32,0},{40,8},{48,16},{56,24},{64,96... | collective-permute-start | bytes 442376 | tf_op jit(solution)/shard_map/ppermute | solution.py:106
  275.4 5.8 %collective-permute-start.10 = (f32[144]{0:T(256)S(1)}, f32[144]{0:T(256)S(1)}, u32[]{:S(2)}, u32[]{:S(2)}) collective-permute-start(f32[144]{0:T(256)S(1)} %convolution_reduce_fusion), channel_id=1, source_target_pairs={{0,1},{1,0},{2,3},{3,2},{4,5},{5,4},{6,7},{7,6},{8,9},{9,8},{10,11... | collective-permute-start | bytes 1736 | tf_op jit(solution)/shard_map/ppermute | solution.py:106
  281.8 4.2 %collective-permute-start.13 = (f32[144]{0:T(256)S(1)}, f32[144]{0:T(256)S(1)}, u32[]{:S(2)}, u32[]{:S(2)}) collective-permute-start(f32[144]{0:T(256)S(1)} %bitcast.167), channel_id=1, source_target_pairs={{0,6},{1,7},{2,4},{3,5},{4,2},{5,3},{6,0},{7,1},{8,14},{9,15},{10,... | collective-permute-start | bytes 1736 | tf_op jit(solution)/shard_map/ppermute | solution.py:106
  282.0 4.0 %collective-permute-start.12 = (f32[144]{0:T(256)S(1)}, f32[144]{0:T(256)S(1)}, u32[]{:S(2)}, u32[]{:S(2)}) collective-permute-start(f32[144]{0:T(256)S(1)} %bitcast.168), channel_id=1, source_target_pairs={{0,4},{1,5},{2,6},{3,7},{4,0},{5,1},{6,2},{7,3},{8,12},{9,13},{10,... | collective-permute-start | bytes 1736 | tf_op jit(solution)/shard_map/ppermute | solution.py:106
  284.0 2.9 collective-permute-start.11
  287.6 3.7 %collective-permute-start.16 = (f32[144]{0:T(256)S(1)}, f32[144]{0:T(256)S(1)}, u32[]{:S(2)}, u32[]{:S(2)}) collective-permute-start(f32[144]{0:T(256)S(1)} %bitcast.163), channel_id=1, source_target_pairs={{0,24},{8,16},{16,8},{24,0},{32,56},{40,48},{48,40},{56,32},{64,88... | collective-permute-start | bytes 1736 | tf_op jit(solution)/shard_map/ppermute | solution.py:106
  288.8 3.9 %collective-permute-start.15 = (f32[144]{0:T(256)S(1)}, f32[144]{0:T(256)S(1)}, u32[]{:S(2)}, u32[]{:S(2)}) collective-permute-start(f32[144]{0:T(256)S(1)} %bitcast.164), channel_id=1, source_target_pairs={{0,16},{8,24},{16,0},{24,8},{32,48},{40,56},{48,32},{56,40},{64,80... | collective-permute-start | bytes 1736 | tf_op jit(solution)/shard_map/ppermute | solution.py:106
  289.5 3.2 collective-permute-start.14
  292.7 3.7 %collective-permute-start.19 = (f32[144]{0:T(256)S(1)}, f32[144]{0:T(256)S(1)}, u32[]{:S(2)}, u32[]{:S(2)}) collective-permute-start(f32[144]{0:T(256)S(1)} %maximum_maximum_fusion.1), channel_id=1, source_target_pairs={{0,96},{8,104},{16,112},{24,120},{32,64},{40,72},{48,80},{56,88},{... | collective-permute-start | bytes 1736 | tf_op jit(solution)/shard_map/ppermute | solution.py:106
  294.9 3.9 %collective-permute-start.18 = (f32[144]{0:T(256)S(1)}, f32[144]{0:T(256)S(1)}, u32[]{:S(2)}, u32[]{:S(2)}) collective-permute-start(f32[144]{0:T(256)S(1)} %maximum_maximum_fusion.1), channel_id=1, source_target_pairs={{0,64},{8,72},{16,80},{24,88},{32,96},{40,104},{48,112},{56,120},{... | collective-permute-start | bytes 1736 | tf_op jit(solution)/shard_map/ppermute | solution.py:106
  295.2 3.5 %collective-permute-start.17 = (f32[144]{0:T(256)S(1)}, f32[144]{0:T(256)S(1)}, u32[]{:S(2)}, u32[]{:S(2)}) collective-permute-start(f32[144]{0:T(256)S(1)} %maximum_maximum_fusion.1), channel_id=1, source_target_pairs={{0,32},{8,40},{16,48},{24,56},{32,0},{40,8},{48,16},{56,24},{64,96... | collective-permute-start | bytes 1736 | tf_op jit(solution)/shard_map/ppermute | solution.py:106
  298.8 30.9 %copy-start.1 = (bf16[384,2048]{1,0:T(8,128)(2,1)S(1)}, bf16[384,2048]{1,0:T(8,128)(2,1)}, u32[]{:S(2)}) copy-start(bf16[384,2048]{1,0:T(8,128)(2,1)} %param.39) | copy-start | bytes 4718596
  (15 other events, 89.8 us)
Sparse Core Ops, SparseCore 0:
  41.4 45.1 all-gather.8
  88.7 82.0 all-gather.4
  173.1 32.0 all-gather.6
  236.7 55.1 reduce-scatter.1
where the time goes:
time: 341 us; the launch traced here: 336 us
  waiting for transfers between devices  127 us (37%)
  matrix products  78.2 us (23%)
  starting transfers between devices  43.1 us (13%)
  local copies, waits for them, and re-layouts  26.2 us (8%)
  blocking collectives  23.8 us (7%)
  other arithmetic  22.4 us (7%)
  between operations  15.3 us (4%)
    all_gather x1, waiting for transfers between devices, shards(): lax.all_gather(pieces.reshape(tok_req, q_cols), 'kv', axis=1, tiled=True)  33.3 us
    ppermute x20, starting transfers between devices, radix_exchange(): got.append(lax.ppermute(value, axis, pairs))  25.5 us
    ppermute x20, waiting for transfers between devices, radix_exchange(): got.append(lax.ppermute(value, axis, pairs))  24.5 us
    all_to_all x1, blocking collectives, regroup(): lax.all_to_all(rows_in, ('req', 'kv'), split_axis=0, concat_axis=0, tiled...  23.8 us
    all_gather x1, waiting for transfers between devices, shards(): rows_all = lax.all_gather(owner_rows, 'kv', axis=0, tiled=True)  23.5 us
    all_to_all x1, waiting for transfers between devices, shards(): lax.all_to_all(jnp.broadcast_to(o_proj[None], (kv_count,) + o_proj.shape)...  20.7 us
    sub x1, matrix products, prefill_full(): expd = jnp.exp(scores - row_peak)  15.9 us
    dot_general x1, matrix products, shards(): jnp.dot(attended, o_full, preferred_element_type=jnp.float32)  14.6 us
  transfers between devices with their start and end apart: 26, of which 19 were waited for; matrix products, arithmetic and copies ran while one was open for 23% of the time, Pallas kernels for 0%

commit v1 on v0

--- a/solution.py
+++ b/solution.py
@@ -182,7 +182,9 @@
     slot_place = lax.dynamic_index_in_dim(slot_table, self_index, 0, keepdims=False) // rows_dev
     arrived = regroup(hidden_in[send_rows])
     owner_rows = arrived[slot_place]
-    rows_all = lax.all_gather(owner_rows, "kv", axis=0, tiled=True)
+    rows_all = jnp.concatenate(
+        lax.all_to_all(jnp.stack([owner_rows] * lax.axis_size("kv")), "kv", 0, 0), axis=0
+    )
     normed = norm_rows(rows_all, attn_gain).astype(jnp.bfloat16)
     o_full = lax.all_to_all(
         jnp.broadcast_to(o_proj[None], (kv_count,) + o_proj.shape),

time: 341 us -> 372 us (1.091)
  waiting for transfers between devices: 127 us -> 149 us
  starting transfers between devices: 43.1 us -> 48.4 us
    all_to_all x0 -> x1, waiting for transfers between devices: none -> 41.6 us  [shards(): lax.all_to_all(jnp.stack([owner_rows] * lax.axis_size('kv')), 'kv', 0, 0)]
    all_gather x1 -> x0, waiting for transfers between devices: 23.5 us -> none  [shards(): rows_all = lax.all_gather(owner_rows, 'kv', axis=0, tiled=True)]
    all_to_all x1, waiting for transfers between devices: 20.7 us -> 41.1 us  [shards(): lax.all_to_all(jnp.broadcast_to(o_proj[None], (kv_count,) + o_proj.shape)...]
    all_gather x1, waiting for transfers between devices: 12.4 us -> 0.01 us  [shards(): weight_all = lax.all_gather(weight_piece, 'req', axis=1, tiled=True)]
    convert_element_type x1 -> x2, other arithmetic: 1.01 us -> 6.59 us  [shards(): normed = norm_rows(rows_all, attn_gain).astype(jnp.bfloat16)]
    all_to_all x0 -> x1, starting transfers between devices: none -> 5.45 us  [shards(): lax.all_to_all(jnp.stack([owner_rows] * lax.axis_size('kv')), 'kv', 0, 0)]
    all_gather x1, waiting for transfers between devices: 33.3 us -> 28.2 us  [shards(): lax.all_gather(pieces.reshape(tok_req, q_cols), 'kv', axis=1, tiled=True)]
    unnamed x49 -> x53, local copies, waits for them, and re-layouts: 4.74 us -> 7.63 us
  transfers between devices with their start and end apart: 26 -> 26, of which waited for: 19 -> 18; matrix products, arithmetic and copies ran while one was open for 23% -> 22% of each run, Pallas kernels for 0% -> 0%
where the time goes in v1:
time: 372 us; the launch traced here: 365 us
  waiting for transfers between devices  149 us (40%)
  matrix products  75.7 us (20%)
  starting transfers between devices  48.4 us (13%)
  local copies, waits for them, and re-layouts  28.1 us (8%)
  other arithmetic  24.7 us (7%)
  blocking collectives  23.8 us (6%)
  between operations  15.3 us (4%)
    all_to_all x1, waiting for transfers between devices, shards(): lax.all_to_all(jnp.stack([owner_rows] * lax.axis_size('kv')), 'kv', 0, 0)  41.6 us
    all_to_all x1, waiting for transfers between devices, shards(): lax.all_to_all(jnp.broadcast_to(o_proj[None], (kv_count,) + o_proj.shape)...  41.1 us
    all_gather x1, waiting for transfers between devices, shards(): lax.all_gather(pieces.reshape(tok_req, q_cols), 'kv', axis=1, tiled=True)  28.2 us
    ppermute x20, starting transfers between devices, radix_exchange(): got.append(lax.ppermute(value, axis, pairs))  25.5 us
    ppermute x20, waiting for transfers between devices, radix_exchange(): got.append(lax.ppermute(value, axis, pairs))  24.6 us
    all_to_all x1, blocking collectives, regroup(): lax.all_to_all(rows_in, ('req', 'kv'), split_axis=0, concat_axis=0, tiled...  23.8 us
    sub x1, matrix products, prefill_full(): expd = jnp.exp(scores - row_peak)  15.5 us
    dot_general x1, matrix products, shards(): jnp.dot(attended, o_full, preferred_element_type=jnp.float32)  14.5 us
  transfers between devices with their start and end apart: 26, of which 18 were waited for; matrix products, arithmetic and copies ran while one was open for 22% of the time, Pallas kernels for 0%

profile of v1, /device:TPU:1, one launch (start us, length us, event | category | flops | bytes accessed | tf_op | source)
XLA Modules:
  0.0 365.1 jit_solution(3081207927116564256)
XLA Ops:
  15.6 11.5 %all-to-all-start = ((bf16[128,2,1024]{2,1,0:T(2,128)(2,1)}), bf16[128,2,1024]{2,1,0:T(2,128)(2,1)S(1)}, u32[]{:S(2)}, u32[]{:S(2)}) async-start(bf16[128,2,1024]{2,1,0:T(2,128)(2,1)} %reshape.597), calls=%async_computation | async-start | bytes 1048576 | tf_op jit(solution)/shard_map/all_to_all | solution.py:147
  27.2 13.7 %all-to-all-done = bf16[128,2,1024]{2,1,0:T(2,128)(2,1)S(1)} async-done(((bf16[128,2,1024]{2,1,0:T(2,128)(2,1)}), bf16[128,2,1024]{2,1,0:T(2,128)(2,1)S(1)}, u32[]{:S(2)}, u32[]{:S(2)}) %all-to-all-start) | async-done | bytes 524320 | tf_op jit(solution)/shard_map/all_to_all | solution.py:147
  42.5 2.6 stack.92
  45.2 5.4 %all-to-all-start.1 = ((bf16[8,128,2048]{2,1,0:T(8,128)(2,1)}), bf16[8,128,2048]{2,1,0:T(8,128)(2,1)}, u32[]{:S(2)}, u32[]{:S(2)}) async-start(bf16[8,128,2048]{2,1,0:T(8,128)(2,1)} %stack.92), calls=%async_computation.1 | async-start | bytes 8388608 | tf_op jit(solution)/shard_map/all_to_all | solution.py:186
  53.9 4.1 %fusion.4 = pred[1016,3064]{1,0:T(8,128)(4,1)} fusion(s32[3064]{0:T(1024)S(1)} %iota_add_fusion, pred[3064]{0:T(1024)(128)(4,1)S(1)} %get-tuple-element.36, pred[3064]{0:T(1024)(128)(4,1)S(1)} %get-tuple-element.37), kind=kLoop, calls=%fused_computation.18 | loop fusion | flops 6226048 | bytes 3131408 | tf_op jit(solution)/shard_map/jit(_where)/select_n | solution.py:45
  58.0 41.6 %all-to-all-done.1 = bf16[8,128,2048]{2,1,0:T(8,128)(2,1)} async-done(((bf16[8,128,2048]{2,1,0:T(8,128)(2,1)}), bf16[8,128,2048]{2,1,0:T(8,128)(2,1)}, u32[]{:S(2)}, u32[]{:S(2)}) %all-to-all-start.1) | async-done | bytes 4194336 | tf_op jit(solution)/shard_map/all_to_all | solution.py:186
  99.5 4.4 %broadcast_in_dim.46 = bf16[8,256,2048]{2,1,0:T(8,128)(2,1)} broadcast(bf16[256,2048]{1,0:T(8,128)(2,1)S(1)} %copy-done.5), dimensions={1,2} | broadcast | bytes 9437184 | tf_op jit(solution)/shard_map/broadcast_in_dim | solution.py:190
  103.9 5.7 %all-to-all-start.2 = ((bf16[8,256,2048]{2,1,0:T(8,128)(2,1)}), bf16[8,256,2048]{2,1,0:T(8,128)(2,1)}, u32[]{:S(2)}, u32[]{:S(2)}) async-start(bf16[8,256,2048]{2,1,0:T(8,128)(2,1)} %broadcast_in_dim.46), calls=%async_computation.2 | async-start | bytes 16777216 | tf_op jit(solution)/shard_map/all_to_all | solution.py:189
  109.8 3.1 fusion.10
  112.9 3.3 fusion.12
  118.1 3.3 fusion.14
  126.7 3.5 fusion.90
  130.8 3.7 %convolution_convert_fusion = bf16[1024,128]{1,0:T(8,128)(2,1)S(1)} fusion(bf16[1024,2048]{1,0:T(8,128)(2,1)} %copy-done.3, bf16[2048,128]{1,0:T(8,128)(2,1)} %param.32), kind=kOutput, calls=%fused_computation.54 | convolution fusion | flops 537001984 | bytes 4980736 | tf_op jit(solution)/shard_map/dot_general | solution.py:213
  135.4 15.5 %fusion.91 = (f32[2,1016]{1,0:T(2,128)S(1)}, f32[2,1016,3064]{2,1,0:T(8,128)}) fusion(pred[1016,3064]{1,0:T(8,128)(4,1)} %fusion.4, bf16[1016,128]{1,0:T(8,128)(2,1)S(1)} %copy.52, bf16[2048,128]{1,0:T(8,128)(2,1)S(1)} %bitcast.193, bf16[1024,2,64]{0,2,1:T(8,128)(2,1)S(1)} %get-tuple-element.15, bf16[1024,2,64]{0,2,1:T(8,128)(2,1)S(1)} %get-tuple-element.14), kind=kOutput, calls=%fused_computation.187 | convolution fusion | flops 1621384704 | bytes 29334016 | tf_op jit(solution)/shard_map/sub | solution.py:48
  150.8 11.6 %fusion.34 = bf16[1016,2,128]{2,0,1:T(8,128)(2,1)S(1)} fusion(f32[2,1016,3064]{2,1,0:T(8,128)} %get-tuple-element.33, f32[2,1016]{1,0:T(2,128)S(1)} %get-tuple-element.32, bf16[1016,128]{1,0:T(8,128)(2,1)S(1)} %slice.142, bf16[2048,128]{1,0:T(8,128)(2,1)S(1)} %bitcast.194), kind=kOutput, calls=%fused_computation.53 | convolution fusion | flops 1608149248 | bytes 26216896 | tf_op jit(solution)/shard_map/gck,kd->cgd/dot_general | solution.py:50
  162.4 41.1 %all-to-all-done.2 = bf16[8,256,2048]{2,1,0:T(8,128)(2,1)} async-done(((bf16[8,256,2048]{2,1,0:T(8,128)(2,1)}), bf16[8,256,2048]{2,1,0:T(8,128)(2,1)}, u32[]{:S(2)}, u32[]{:S(2)}) %all-to-all-start.2) | async-done | bytes 8388640 | tf_op jit(solution)/shard_map/all_to_all | solution.py:189
  204.6 28.2 %all-gather.5.cloned.1.call-done = bf16[1024,2048]{0,1:T(8,128)(2,1)} async-done(((bf16[1024,256]{0,1:T(8,128)(2,1)}), bf16[1024,2048]{0,1:T(8,128)(2,1)}) %all-gather.5.cloned.1.call-update) | async-done | bytes 4194320 | tf_op jit(solution)/shard_map/all_gather | solution.py:254
  232.9 14.5 %fusion.7 = (f32[1024]{0:T(1024)S(1)}, bf16[1024,2048]{1,0:T(8,128)(2,1)S(1)}) fusion(bf16[1024,2048]{0,1:T(8,128)(2,1)} %all-gather.5.cloned.1.call-done, bf16[2048,2048]{1,0:T(8,128)(2,1)} %bitcast.30, bf16[8,128,2048]{2,1,0:T(8,128)(2,1)} %all-to-all-done.1), kind=kOutput, calls=%fused_computation.23 | convolution fusion | flops 8602516480 | bytes 20975616 | tf_op jit(solution)/shard_map/dot_general | solution.py:256
  247.4 7.0 %fusion.20 = f32[1024,768]{1,0:T(8,128)S(1)} fusion(bf16[3,768,2048]{2,1,0:T(8,128)(2,1)} %all-gather.3.cloned.1.call-done, bf16[1024,2048]{1,0:T(8,128)(2,1)S(1)} %get-tuple-element.35, f32[2048]{0:T(1024)S(1)} %copy-done.19, f32[1024]{0:T(1024)S(1)} %add_rsqrt_fusion.1), kind=kOutput, calls=%fused_computation.40 | convolution fusion | flops 3229614080 | bytes 10498048 | tf_op jit(solution)/shard_map/dot_general | solution.py:261
  254.5 3.9 %multiply_convert_fusion = bf16[1024,768]{1,0:T(8,128)(2,1)S(1)} fusion(f32[1024,768]{1,0:T(8,128)S(1)} %fusion.20, bf16[3,768,2048]{2,1,0:T(8,128)(2,1)S(1)} %bitcast.162, bf16[1024,2048]{1,0:T(8,128)(2,1)S(1)} %get-tuple-element.35, f32[2048]{0:T(1024)S(1)} %copy-done.19, f32[1024]{0:T(1024)S(1)} %add_rsqrt_fusion.1), kind=kOutput, calls=%fused_computation.44 | convolution fusion | flops 3234332672 | bytes 12070912 | tf_op jit(solution)/shard_map/dot_general | solution.py:260
  259.6 5.6 %fusion.18 = f32[1024,2048]{1,0:T(8,128)} fusion(bf16[1024,768]{1,0:T(8,128)(2,1)S(1)} %multiply_convert_fusion, bf16[3,768,2048]{2,1,0:T(8,128)(2,1)S(1)} %bitcast.162), kind=kOutput, calls=%fused_computation.38 | convolution fusion | flops 3221225472 | bytes 13107200 | tf_op jit(solution)/shard_map/dot_general | solution.py:265
  265.3 2.4 fusion.16
  273.2 6.2 %collective-permute-done.3 = f32[16,2048]{1,0:T(8,128)S(1)} collective-permute-done((f32[16,2048]{1,0:T(8,128)S(1)}, f32[16,2048]{1,0:T(8,128)S(1)}, u32[]{:S(2)}, u32[]{:S(2)}) %collective-permute-start.3) | collective-permute-done | bytes 131104 | tf_op jit(solution)/shard_map/ppermute | solution.py:106
  282.6 2.5 collective-permute-start.6
  287.4 2.5 collective-permute-done.5
  290.6 2.8 collective-permute-start.9
  294.1 3.3 collective-permute-done.9
  299.9 4.3 %convolution_reduce_fusion = f32[144]{0:T(256)S(1)} fusion(bf16[144,2048]{1,0:T(8,128)(2,1)S(1)} %reshape.506, bf16[2048,1187]{0,1:T(8,128)(2,1)} %param.41), kind=kOutput, calls=%fused_computation.55 | convolution fusion | flops 700291840 | bytes 5452352 | tf_op jit(solution)/shard_map/dot_general | solution.py:274
  304.2 5.0 %collective-permute-start.10 = (f32[144]{0:T(256)S(1)}, f32[144]{0:T(256)S(1)}, u32[]{:S(2)}, u32[]{:S(2)}) collective-permute-start(f32[144]{0:T(256)S(1)} %convolution_reduce_fusion), channel_id=1, source_target_pairs={{0,1},{1,0},{2,3},{3,2},{4,5},{5,4},{6,7},{7,6},{8,9},{9,8},{10,11... | collective-permute-start | bytes 1736 | tf_op jit(solution)/shard_map/ppermute | solution.py:106
  328.1 2.3 scatter_custom_fusion
  331.7 23.8 %all_to_all.34 = bf16[128,2,1024]{2,1,0:T(2,128)(2,1)S(1)} all-to-all(bf16[128,2,1024]{2,1,0:T(2,128)(2,1)S(1)} %reshape.599), channel_id=1, replica_groups=mesh['req'=16,'kv'=8] {'req','kv'}, dimensions={0} | all-to-all | bytes 1048576 | tf_op jit(solution)/shard_map/all_to_all | solution.py:147
  356.0 2.4 scatter_custom_fusion.1
  (182 shorter events, 59.1 us)
Async XLA Ops:
  7.2 196.3 %all-gather.3.cloned.1.call-start = ((), (), s32[]{:S(2)}) async-start(), calls=%async_computation.5 | async-start | bytes 10027008 | tf_op jit(solution)/shard_map/all_gather | solution.py:205
  15.6 25.2 %all-to-all-start = ((bf16[128,2,1024]{2,1,0:T(2,128)(2,1)}), bf16[128,2,1024]{2,1,0:T(2,128)(2,1)S(1)}, u32[]{:S(2)}, u32[]{:S(2)}) async-start(bf16[128,2,1024]{2,1,0:T(2,128)(2,1)} %reshape.597), calls=%async_computation | async-start | bytes 1048576 | tf_op jit(solution)/shard_map/all_to_all | solution.py:147
  45.2 54.4 %all-to-all-start.1 = ((bf16[8,128,2048]{2,1,0:T(8,128)(2,1)}), bf16[8,128,2048]{2,1,0:T(8,128)(2,1)}, u32[]{:S(2)}, u32[]{:S(2)}) async-start(bf16[8,128,2048]{2,1,0:T(8,128)(2,1)} %stack.92), calls=%async_computation.1 | async-start | bytes 8388608 | tf_op jit(solution)/shard_map/all_to_all | solution.py:186
  50.6 48.9 %copy-start.5 = (bf16[256,2048]{1,0:T(8,128)(2,1)S(1)}, bf16[256,2048]{1,0:T(8,128)(2,1)}, u32[]{:S(2)}) copy-start(bf16[256,2048]{1,0:T(8,128)(2,1)} %param.35) | copy-start | bytes 3145732
  103.9 99.6 %all-to-all-start.2 = ((bf16[8,256,2048]{2,1,0:T(8,128)(2,1)}), bf16[8,256,2048]{2,1,0:T(8,128)(2,1)}, u32[]{:S(2)}, u32[]{:S(2)}) async-start(bf16[8,256,2048]{2,1,0:T(8,128)(2,1)} %broadcast_in_dim.46), calls=%async_computation.2 | async-start | bytes 16777216 | tf_op jit(solution)/shard_map/all_to_all | solution.py:189
  109.6 123.2 %all-gather.5.cloned.1.call-start = ((), (), s32[]{:S(2)}) async-start(), calls=%async_computation.6 | async-start | bytes 4718592 | tf_op jit(solution)/shard_map/all_gather | solution.py:254
  204.5 42.9 %copy-start.19 = (f32[2048]{0:T(1024)S(1)}, f32[2048]{0:T(1024)}, u32[]{:S(2)}) copy-start(f32[2048]{0:T(1024)} %param.36) | copy-start | bytes 24580
  204.6 123.5 %reduce-scatter.2.cloned.1.call-start = ((), (), s32[]{:S(2)}) async-start(), calls=%async_computation.7 | async-start | bytes 9437184 | tf_op jit(solution)/shard_map/reduce_scatter | solution.py:266
  232.8 21.6 %slice-start = ((s8[9437184]{0:T(1024)(128)(4,1)}), s8[1048576]{0:T(1024)(128)(4,1)S(1)}, s32[]{:S(2)}) async-start(s8[9437184]{0:T(1024)(128)(4,1)} %bitcast.161), calls=%async_computation.8 | async-start | bytes 2097152
  232.9 21.6 %slice-start.1 = ((s8[9437184]{0:T(1024)(128)(4,1)}), s8[4194304]{0:T(1024)(128)(4,1)S(1)}, s32[]{:S(2)}) async-start(s8[9437184]{0:T(1024)(128)(4,1)} %bitcast.161), calls=%async_computation.9 | async-start | bytes 8388608
  265.3 17.2 %copy-start.12 = (f32[2048]{0:T(1024)S(1)}, f32[2048]{0:T(1024)}, u32[]{:S(2)}) copy-start(f32[2048]{0:T(1024)} %param.40) | copy-start | bytes 24580
  267.8 1.5 collective-permute-start
  269.9 9.6 %collective-permute-start.3 = (f32[16,2048]{1,0:T(8,128)S(1)}, f32[16,2048]{1,0:T(8,128)S(1)}, u32[]{:S(2)}, u32[]{:S(2)}) collective-permute-start(f32[16,2048]{1,0:T(8,128)S(1)} %fusion.110), channel_id=1, source_target_pairs={{0,6},{1,7},{2,4},{3,5},{4,2},{5,3},{6,0},{7,1},{8,14},{9,15},{10,... | collective-permute-start | bytes 393224 | tf_op jit(solution)/shard_map/ppermute | solution.py:106
  270.5 9.0 %collective-permute-start.2 = (f32[16,2048]{1,0:T(8,128)S(1)}, f32[16,2048]{1,0:T(8,128)S(1)}, u32[]{:S(2)}, u32[]{:S(2)}) collective-permute-start(f32[16,2048]{1,0:T(8,128)S(1)} %fusion.110), channel_id=1, source_target_pairs={{0,4},{1,5},{2,6},{3,7},{4,0},{5,1},{6,2},{7,3},{8,12},{9,13},{10,... | collective-permute-start | bytes 393224 | tf_op jit(solution)/shard_map/ppermute | solution.py:106
  271.9 8.9 %collective-permute-start.1 = (f32[16,2048]{1,0:T(8,128)S(1)}, f32[16,2048]{1,0:T(8,128)S(1)}, u32[]{:S(2)}, u32[]{:S(2)}) collective-permute-start(f32[16,2048]{1,0:T(8,128)S(1)} %fusion.110), channel_id=1, source_target_pairs={{0,2},{1,3},{2,0},{3,1},{4,6},{5,7},{6,4},{7,5},{8,10},{9,11},{10,... | collective-permute-start | bytes 393224 | tf_op jit(solution)/shard_map/ppermute | solution.py:106
  282.6 4.8 %collective-permute-start.6 = (bf16[9,2048]{1,0:T(8,128)(2,1)S(1)}, bf16[9,2048]{1,0:T(8,128)(2,1)S(1)}, u32[]{:S(2)}, u32[]{:S(2)}) collective-permute-start(bf16[9,2048]{1,0:T(8,128)(2,1)S(1)} %fusion.57), channel_id=1, source_target_pairs={{0,24},{8,16},{16,8},{24,0},{32,56},{40,48},{48,40},{56,32},{64,88... | collective-permute-start | bytes 110600 | tf_op jit(solution)/shard_map/ppermute | solution.py:106
  285.1 4.7 %collective-permute-start.5 = (bf16[9,2048]{1,0:T(8,128)(2,1)S(1)}, bf16[9,2048]{1,0:T(8,128)(2,1)S(1)}, u32[]{:S(2)}, u32[]{:S(2)}) collective-permute-start(bf16[9,2048]{1,0:T(8,128)(2,1)S(1)} %fusion.57), channel_id=1, source_target_pairs={{0,16},{8,24},{16,0},{24,8},{32,48},{40,56},{48,32},{56,40},{64,80... | collective-permute-start | bytes 110600 | tf_op jit(solution)/shard_map/ppermute | solution.py:106
  285.7 4.2 %collective-permute-start.4 = (bf16[9,2048]{1,0:T(8,128)(2,1)S(1)}, bf16[9,2048]{1,0:T(8,128)(2,1)S(1)}, u32[]{:S(2)}, u32[]{:S(2)}) collective-permute-start(bf16[9,2048]{1,0:T(8,128)(2,1)S(1)} %fusion.57), channel_id=1, source_target_pairs={{0,8},{8,0},{16,24},{24,16},{32,40},{40,32},{48,56},{56,48},{64,72... | collective-permute-start | bytes 110600 | tf_op jit(solution)/shard_map/ppermute | solution.py:106
  290.6 6.8 %collective-permute-start.9 = (bf16[36,2048]{1,0:T(8,128)(2,1)S(1)}, bf16[36,2048]{1,0:T(8,128)(2,1)S(1)}, u32[]{:S(2)}, u32[]{:S(2)}) collective-permute-start(bf16[36,2048]{1,0:T(8,128)(2,1)S(1)} %reshape.505), channel_id=1, source_target_pairs={{0,96},{8,104},{16,112},{24,120},{32,64},{40,72},{48,80},{56,88},{... | collective-permute-start | bytes 442376 | tf_op jit(solution)/shard_map/ppermute | solution.py:106
  293.3 5.8 %collective-permute-start.8 = (bf16[36,2048]{1,0:T(8,128)(2,1)S(1)}, bf16[36,2048]{1,0:T(8,128)(2,1)S(1)}, u32[]{:S(2)}, u32[]{:S(2)}) collective-permute-start(bf16[36,2048]{1,0:T(8,128)(2,1)S(1)} %reshape.505), channel_id=1, source_target_pairs={{0,64},{8,72},{16,80},{24,88},{32,96},{40,104},{48,112},{56,120},{... | collective-permute-start | bytes 442376 | tf_op jit(solution)/shard_map/ppermute | solution.py:106
  293.7 5.4 %collective-permute-start.7 = (bf16[36,2048]{1,0:T(8,128)(2,1)S(1)}, bf16[36,2048]{1,0:T(8,128)(2,1)S(1)}, u32[]{:S(2)}, u32[]{:S(2)}) collective-permute-start(bf16[36,2048]{1,0:T(8,128)(2,1)S(1)} %reshape.505), channel_id=1, source_target_pairs={{0,32},{8,40},{16,48},{24,56},{32,0},{40,8},{48,16},{56,24},{64,96... | collective-permute-start | bytes 442376 | tf_op jit(solution)/shard_map/ppermute | solution.py:106
  304.2 5.8 %collective-permute-start.10 = (f32[144]{0:T(256)S(1)}, f32[144]{0:T(256)S(1)}, u32[]{:S(2)}, u32[]{:S(2)}) collective-permute-start(f32[144]{0:T(256)S(1)} %convolution_reduce_fusion), channel_id=1, source_target_pairs={{0,1},{1,0},{2,3},{3,2},{4,5},{5,4},{6,7},{7,6},{8,9},{9,8},{10,11... | collective-permute-start | bytes 1736 | tf_op jit(solution)/shard_map/ppermute | solution.py:106
  310.6 4.2 %collective-permute-start.13 = (f32[144]{0:T(256)S(1)}, f32[144]{0:T(256)S(1)}, u32[]{:S(2)}, u32[]{:S(2)}) collective-permute-start(f32[144]{0:T(256)S(1)} %bitcast.185), channel_id=1, source_target_pairs={{0,6},{1,7},{2,4},{3,5},{4,2},{5,3},{6,0},{7,1},{8,14},{9,15},{10,... | collective-permute-start | bytes 1736 | tf_op jit(solution)/shard_map/ppermute | solution.py:106
  310.7 4.0 %collective-permute-start.12 = (f32[144]{0:T(256)S(1)}, f32[144]{0:T(256)S(1)}, u32[]{:S(2)}, u32[]{:S(2)}) collective-permute-start(f32[144]{0:T(256)S(1)} %bitcast.186), channel_id=1, source_target_pairs={{0,4},{1,5},{2,6},{3,7},{4,0},{5,1},{6,2},{7,3},{8,12},{9,13},{10,... | collective-permute-start | bytes 1736 | tf_op jit(solution)/shard_map/ppermute | solution.py:106
  312.8 2.9 collective-permute-start.11
  316.3 3.7 %collective-permute-start.16 = (f32[144]{0:T(256)S(1)}, f32[144]{0:T(256)S(1)}, u32[]{:S(2)}, u32[]{:S(2)}) collective-permute-start(f32[144]{0:T(256)S(1)} %bitcast.181), channel_id=1, source_target_pairs={{0,24},{8,16},{16,8},{24,0},{32,56},{40,48},{48,40},{56,32},{64,88... | collective-permute-start | bytes 1736 | tf_op jit(solution)/shard_map/ppermute | solution.py:106
  317.5 3.9 %collective-permute-start.15 = (f32[144]{0:T(256)S(1)}, f32[144]{0:T(256)S(1)}, u32[]{:S(2)}, u32[]{:S(2)}) collective-permute-start(f32[144]{0:T(256)S(1)} %bitcast.182), channel_id=1, source_target_pairs={{0,16},{8,24},{16,0},{24,8},{32,48},{40,56},{48,32},{56,40},{64,80... | collective-permute-start | bytes 1736 | tf_op jit(solution)/shard_map/ppermute | solution.py:106
  318.2 3.2 collective-permute-start.14
  321.4 3.7 %collective-permute-start.19 = (f32[144]{0:T(256)S(1)}, f32[144]{0:T(256)S(1)}, u32[]{:S(2)}, u32[]{:S(2)}) collective-permute-start(f32[144]{0:T(256)S(1)} %maximum_maximum_fusion.1), channel_id=1, source_target_pairs={{0,96},{8,104},{16,112},{24,120},{32,64},{40,72},{48,80},{56,88},{... | collective-permute-start | bytes 1736 | tf_op jit(solution)/shard_map/ppermute | solution.py:106
  323.6 3.9 %collective-permute-start.18 = (f32[144]{0:T(256)S(1)}, f32[144]{0:T(256)S(1)}, u32[]{:S(2)}, u32[]{:S(2)}) collective-permute-start(f32[144]{0:T(256)S(1)} %maximum_maximum_fusion.1), channel_id=1, source_target_pairs={{0,64},{8,72},{16,80},{24,88},{32,96},{40,104},{48,112},{56,120},{... | collective-permute-start | bytes 1736 | tf_op jit(solution)/shard_map/ppermute | solution.py:106
  323.9 3.5 collective-permute-start.17
  327.5 30.9 %copy-start.1 = (bf16[384,2048]{1,0:T(8,128)(2,1)S(1)}, bf16[384,2048]{1,0:T(8,128)(2,1)}, u32[]{:S(2)}) copy-start(bf16[384,2048]{1,0:T(8,128)(2,1)} %param.39) | copy-start | bytes 4718596
  (17 other events, 79.7 us)
Sparse Core Ops, SparseCore 0:
  12.0 84.5 all-gather.2
  204.7 28.1 all-gather.4
  265.3 55.1 reduce-scatter.1
